TPU v7x, 32 devices: a whole 2x2x4 slice. The times are simulated.
32 devices in a mesh: groups: 2 (over x), ctx: 8 (over z, y), head: 2 (over core).
Axes of the slice: x: 2, y: 2, z: 4, core: 2. Of those that a mesh axis runs over, the one named last changes fastest.
Arguments:
- queries: bfloat16 [4096, 2048], P(('groups', 'ctx'), 'head'), parts along dimension 0, may hold values from -12 to 12
- span_keys: bfloat16 [4096, 2048], P(('groups', 'ctx'), 'head'), parts along dimension 0, may hold values from -12 to 12
- span_values: bfloat16 [4096, 2048], P(('groups', 'ctx'), 'head'), parts along dimension 0, may hold values from -6 to 6
- cache_keys: bfloat16 [8192, 2048], P(('groups', 'ctx'), 'head'), parts along dimension 0, may hold values from -12 to 12
- cache_values: bfloat16 [8192, 2048], P(('groups', 'ctx'), 'head'), parts along dimension 0, may hold values from -6 to 6
- routes: int32 [2, 32, 8, 4], P('head', ('groups', 'ctx')), parts along dimension 1, may hold values from 0 to 7, all different within a row; in each aligned block of 16 rows (0 to 15, 16 to 31, ..., all dimensions but the last counted through in order) at most 16 rows name the same one
- out_weight: bfloat16 [2048, 4096], P('head'), may hold values from -0.125 to 0.125
Outputs:
- projected: bfloat16 [4096, 4096], P(('groups', 'ctx'), 'head'), parts along dimension 0
There are 2 independent parts, one for each index of `groups`. A program takes and returns all parts, laid end to end along the dimension named above; an argument that names none is the same for every part. Nothing has to cross between parts.
Inputs may be any that keep to these rules, and one draw needn't show every extreme that they name: `routes`: each row names 4 different key blocks; among the 16 rows of one device no key block is named more than 16 times.
All inputs are finite; a program needn't handle non-finite values.
Results may differ from a plain program's by a relative error of at most 0.0064.
Values may be sent and summed in bfloat16 or wider, within the bound.
A program may use at most 128 MiB of HBM per device.

v0:
```python
import math
import jax
import jax.numpy as jnp
from jax import lax
from jax.sharding import PartitionSpec as P

DH = 128
QB = 128


def shortened(value):

    def short(part):
        return part.astype(jnp.bfloat16) if part.dtype == jnp.float32 else part

    return jax.tree.map(short, value)


def soft_partial(scores, values_block, pattern):
    highest = jnp.max(scores, axis=-1, keepdims=True)
    exponent = jnp.exp(scores - highest)
    denominator = jnp.sum(exponent, axis=-1, keepdims=True)
    weights_low = (exponent / denominator).astype(jnp.bfloat16)
    result = jnp.einsum(
        pattern, weights_low, values_block, preferred_element_type=jnp.float32
    ).astype(jnp.bfloat16)
    log_total = highest[..., 0] + jnp.log(denominator[..., 0])
    return (result, log_total)


def on_device(queries, span_keys, span_values, cache_keys, cache_values, routes, out_weight):
    blocks = routes.shape[1]
    heads_here = routes.shape[2]
    top_picks = routes.shape[3]
    key_rows = cache_keys.shape[0]
    devices = lax.axis_size("ctx")
    scaling = 1.0 / math.sqrt(DH)
    blocked = queries.reshape(blocks, QB, heads_here, DH)
    most_rows = max(2, 2 * blocks * heads_here * top_picks // devices)
    groups = 1
    per_peer = groups * most_rows
    slot_total = per_peer * devices
    wanted = routes.reshape(-1)
    item_count = wanted.shape[0]
    item_ids = jnp.arange(item_count, dtype=jnp.int32)
    block_of = item_ids // (heads_here * top_picks)
    head_of = item_ids // top_picks % heads_here
    bucket = wanted * groups + block_of % groups
    one_hot = (bucket[:, None] == jnp.arange(devices * groups, dtype=jnp.int32)[None, :]).astype(
        jnp.int32
    )
    ranking = jnp.sum(jnp.cumsum(one_hot, axis=0) * one_hot, axis=1) - 1
    position = (block_of % groups * most_rows + ranking) * devices + wanted
    matches = position[None, :] == jnp.arange(slot_total, dtype=jnp.int32)[:, None]
    filled = jnp.any(matches, axis=1)
    source = jnp.sum(jnp.where(matches, item_ids[None, :], 0), axis=1)
    gathered = blocked[block_of[source], :, head_of[source], :]
    slot_queries = jnp.where(filled[:, None, None], gathered, jnp.zeros_like(gathered)).reshape(
        per_peer, devices, QB, DH
    )
    slot_heads = jnp.where(filled, head_of[source], 0).reshape(per_peer, devices)
    keys_by_head = cache_keys.reshape(key_rows, heads_here, DH).transpose(1, 0, 2)
    values_by_head = cache_values.reshape(key_rows, heads_here, DH).transpose(1, 0, 2)

    def one_portion(portion):
        queried, head_ids = portion
        chosen_keys = keys_by_head[head_ids]
        chosen_values = values_by_head[head_ids]
        scores = (
            jnp.einsum("pqd,pkd->pqk", queried, chosen_keys, preferred_element_type=jnp.float32)
            * scaling
        )
        return soft_partial(scores, chosen_values, "pqk,pkd->pqd")

    outputs, log_sums = lax.map(
        one_portion,
        (
            lax.all_to_all(slot_queries, "ctx", split_axis=1, concat_axis=1, tiled=True),
            lax.all_to_all(slot_heads, "ctx", split_axis=1, concat_axis=1, tiled=True),
        ),
    )
    outputs_back = jax.tree.map(
        lambda part, own: part.astype(own.dtype),
        lax.all_to_all(shortened(outputs), "ctx", split_axis=1, concat_axis=1, tiled=True),
        outputs,
    )
    sums_back = lax.all_to_all(log_sums, "ctx", split_axis=1, concat_axis=1, tiled=True)
    routed_out = outputs_back.reshape(slot_total, QB, DH)[position].reshape(
        blocks, heads_here, top_picks, QB, DH
    )
    routed_lse = sums_back.reshape(slot_total, QB)[position].reshape(
        blocks, heads_here, top_picks, QB
    )
    own_keys = span_keys.reshape(blocks, QB, heads_here, DH)
    own_values = span_values.reshape(blocks, QB, heads_here, DH)
    causal = jnp.arange(QB)[:, None] >= jnp.arange(QB)[None, :]
    self_scores = (
        jnp.einsum("bqhd,bkhd->bhqk", blocked, own_keys, preferred_element_type=jnp.float32)
        * scaling
    )
    self_scores = jnp.where(causal[None, None], self_scores, -jnp.inf)
    self_out, self_lse = soft_partial(self_scores, own_values, "bhqk,bkhd->bhqd")
    all_lse = jnp.concatenate([routed_lse, self_lse[:, :, None]], axis=2)
    all_out = jnp.concatenate(
        [routed_out.astype(jnp.float32), self_out[:, :, None].astype(jnp.float32)], axis=2
    )
    highest = jnp.max(all_lse, axis=2, keepdims=True)
    merge_weights = jnp.exp(all_lse - highest)
    merge_weights = merge_weights / jnp.sum(merge_weights, axis=2, keepdims=True)
    attention = jnp.sum(merge_weights[..., None] * all_out, axis=2)
    attention = (
        attention.transpose(0, 2, 1, 3).reshape(blocks * QB, heads_here * DH).astype(jnp.bfloat16)
    )
    partial_sums = jnp.dot(attention, out_weight, preferred_element_type=jnp.float32)
    return lax.psum_scatter(partial_sums, "head", scatter_dimension=1, tiled=True).astype(
        jnp.bfloat16
    )


def solution(mesh):
    placed = (
        P(("groups", "ctx"), "head"),
        P(("groups", "ctx"), "head"),
        P(("groups", "ctx"), "head"),
        P(("groups", "ctx"), "head"),
        P(("groups", "ctx"), "head"),
        P("head", ("groups", "ctx"), None, None),
        P("head", None),
    )
    return jax.shard_map(
        on_device,
        mesh=mesh,
        in_specs=placed,
        out_specs=P(("groups", "ctx"), "head"),
        check_vma=False,
    )
```

profile of v0, /device:TPU:0, one launch (start us, length us, event | category | flops | bytes accessed | tf_op | source)
XLA Modules:
  0.0 391.5 jit_solution(3078422564545863952)
XLA Ops:
  10.0 7.3 %all-to-all-start.1 = ((s32[16,8,1]{0,2,1:T(1,128)}), s32[16,8,1]{0,2,1:T(1,128)S(1)}, u32[]{:S(2)}, u32[]{:S(2)}) async-start(s32[16,8,1]{0,2,1:T(1,128)} %copy.97), calls=%async_computation.1 | async-start | bytes 8192 | tf_op jit(solution)/shard_map/all_to_all | solution.py:79
  20.8 3.1 gather_fusion.4
  23.8 3.8 copy_select_fusion
  27.6 6.1 %all-to-all-start = ((bf16[16,8,128,128]{3,2,0,1:T(8,128)(2,1)}), bf16[16,8,128,128]{3,2,0,1:T(8,128)(2,1)}, u32[]{:S(2)}, u32[]{:S(2)}) async-start(bf16[16,8,128,128]{3,2,0,1:T(8,128)(2,1)} %copy_select_fusion), calls=%async_computation | async-start | bytes 8388608 | tf_op jit(solution)/shard_map/all_to_all | solution.py:78
  37.6 88.9 %all-to-all-done = bf16[16,8,128,128]{3,2,0,1:T(8,128)(2,1)} async-done(((bf16[16,8,128,128]{3,2,0,1:T(8,128)(2,1)}), bf16[16,8,128,128]{3,2,0,1:T(8,128)(2,1)}, u32[]{:S(2)}, u32[]{:S(2)}) %all-to-all-start) | async-done | bytes 4194336 | tf_op jit(solution)/shard_map/all_to_all | solution.py:78
  126.5 119.4 %while.13 = (s32[]{:T(128)}, bf16[16,8,128,128]{3,2,0,1:T(8,128)(2,1)}, f32[16,8,128]{2,0,1:T(8,128)S(1)}, bf16[16,8,128,128]{3,2,0,1:T(8,128)(2,1)}, s32[16,8]{...) while((s32[]{:T(128)}, bf16[16,8,128,128]{3,2,0,1:T(8,128)(2,1)}, ...), condition=%wide.region_7.8_spmd.clone, body=%wide.region_4.7_spmd.sunk.clone | while | flops 273285152 | bytes 13153525 | solution.py:75
  126.5 2.0 gather_fusion.1
  130.5 2.0 gather_fusion
  133.9 2.0 gather_fusion.1
  138.0 2.0 gather_fusion
  141.4 2.0 gather_fusion.1
  145.4 2.0 gather_fusion
  148.8 2.0 gather_fusion.1
  152.9 2.0 gather_fusion
  156.3 2.0 gather_fusion.1
  160.3 2.0 gather_fusion
  163.8 2.0 gather_fusion.1
  165.7 1.5 multiply_reduce_fusion.4
  167.8 2.0 gather_fusion
  171.2 2.0 gather_fusion.1
  175.3 2.0 gather_fusion
  178.7 2.0 gather_fusion.1
  182.7 2.0 gather_fusion
  186.1 2.0 gather_fusion.1
  190.2 2.0 gather_fusion
  193.6 2.0 gather_fusion.1
  197.6 2.0 gather_fusion
  201.1 2.0 gather_fusion.1
  205.1 2.0 gather_fusion
  208.5 2.0 gather_fusion.1
  212.6 2.0 gather_fusion
  216.0 2.0 gather_fusion.1
  220.0 2.0 gather_fusion
  223.5 2.0 gather_fusion.1
  227.5 2.0 gather_fusion
  230.9 2.0 gather_fusion.1
  235.0 2.0 gather_fusion
  238.4 2.0 gather_fusion.1
  242.5 2.0 gather_fusion
  245.8 10.3 %all_to_all.24 = f32[16,8,128]{2,0,1:T(8,128)S(1)} all-to-all(f32[16,8,128]{2,0,1:T(8,128)S(1)} %get-tuple-element.43), channel_id=1, replica_groups=mesh['groups'=2,'ctx'=8,'head'=2] {'ctx'}, dimensions={1} | all-to-all | bytes 131072 | tf_op jit(solution)/shard_map/all_to_all | solution.py:87
  256.2 4.7 %all-to-all-start.3 = ((bf16[16,8,128,128]{3,2,0,1:T(8,128)(2,1)}), bf16[16,8,128,128]{3,2,0,1:T(8,128)(2,1)}, u32[]{:S(2)}, u32[]{:S(2)}) async-start(bf16[16,8,128,128]{3,2,0,1:T(8,128)(2,1)} %get-tuple-element.44), calls=%async_computation.3 | async-start | bytes 8388608 | tf_op jit(solution)/shard_map/all_to_all | solution.py:84
  263.7 89.5 %all-to-all-done.3 = bf16[16,8,128,128]{3,2,0,1:T(8,128)(2,1)} async-done(((bf16[16,8,128,128]{3,2,0,1:T(8,128)(2,1)}), bf16[16,8,128,128]{3,2,0,1:T(8,128)(2,1)}, u32[]{:S(2)}, u32[]{:S(2)}) %all-to-all-start.3) | async-done | bytes 4194336 | tf_op jit(solution)/shard_map/all_to_all | solution.py:84
  353.2 4.7 %copy.112 = bf16[16,8,128,128]{3,2,1,0:T(8,128)(2,1)} copy(bf16[16,8,128,128]{3,2,0,1:T(8,128)(2,1)} %all-to-all-done.3) | data formatting | bytes 8388608 | tf_op jit(solution)/shard_map/all_to_all | solution.py:84
  357.9 3.1 gather_fusion.6
  361.1 1.8 multiply_reduce_fusion.1
  363.2 7.6 %fusion.15 = f32[256,4096]{1,0:T(8,128)} fusion(bf16[1024,4096]{1,0:T(8,128)(2,1)} %param.15, bf16[32,8,8,128]{3,2,1,0:T(8,128)(2,1)S(1)} %bitcast.116), kind=kOutput, calls=%fused_computation.36 | convolution fusion | flops 2147483648 | bytes 13107200 | tf_op jit(solution)/shard_map/dot_general | solution.py:114
  370.9 11.1 %reduce-scatter.2.cloned.1.call-done = f32[256,2048]{1,0:T(8,128)} async-done(((f32[256,4096]{1,0:T(8,128)}), f32[256,2048]{1,0:T(8,128)}) %reduce-scatter.2.cloned.1.call-update) | async-done | bytes 2097168 | tf_op jit(solution)/shard_map/reduce_scatter | solution.py:115
  382.0 2.7 convert_element_type.43
  (170 shorter events, 67.5 us)
Async XLA Ops:
  10.0 17.6 %all-to-all-start.1 = ((s32[16,8,1]{0,2,1:T(1,128)}), s32[16,8,1]{0,2,1:T(1,128)S(1)}, u32[]{:S(2)}, u32[]{:S(2)}) async-start(s32[16,8,1]{0,2,1:T(1,128)} %copy.97), calls=%async_computation.1 | async-start | bytes 8192 | tf_op jit(solution)/shard_map/all_to_all | solution.py:79
  19.8 0.8 copy-start
  27.6 6.2 %copy-start.2 = (bf16[512,1024]{1,0:T(8,128)(2,1)S(1)}, bf16[512,1024]{1,0:T(8,128)(2,1)}, u32[]{:S(2)}) copy-start(bf16[512,1024]{1,0:T(8,128)(2,1)} %param.12) | copy-start | bytes 3145732
  27.6 98.9 %all-to-all-start = ((bf16[16,8,128,128]{3,2,0,1:T(8,128)(2,1)}), bf16[16,8,128,128]{3,2,0,1:T(8,128)(2,1)}, u32[]{:S(2)}, u32[]{:S(2)}) async-start(bf16[16,8,128,128]{3,2,0,1:T(8,128)(2,1)} %copy_select_fusion), calls=%async_computation | async-start | bytes 8388608 | tf_op jit(solution)/shard_map/all_to_all | solution.py:78
  33.7 1.9 copy-start.3
  256.2 4.8 %copy-start.4 = (bf16[256,1024]{1,0:T(8,128)(2,1)S(1)}, bf16[256,1024]{1,0:T(8,128)(2,1)}, u32[]{:S(2)}) copy-start(bf16[256,1024]{1,0:T(8,128)(2,1)} %param.10) | copy-start | bytes 1572868
  256.2 4.9 %copy-start.5 = (bf16[256,1024]{1,0:T(8,128)(2,1)S(1)}, bf16[256,1024]{1,0:T(8,128)(2,1)}, u32[]{:S(2)}) copy-start(bf16[256,1024]{1,0:T(8,128)(2,1)} %param.11) | copy-start | bytes 1572868
  256.2 5.1 %copy-start.1 = (bf16[32,8,8,128]{3,2,1,0:T(8,128)(2,1)S(1)}, bf16[32,8,8,128]{3,2,1,0:T(8,128)(2,1)}, u32[]{:S(2)}) copy-start(bf16[32,8,8,128]{3,2,1,0:T(8,128)(2,1)} %copy-done) | copy-start | bytes 1572868
  256.2 97.0 %all-to-all-start.3 = ((bf16[16,8,128,128]{3,2,0,1:T(8,128)(2,1)}), bf16[16,8,128,128]{3,2,0,1:T(8,128)(2,1)}, u32[]{:S(2)}, u32[]{:S(2)}) async-start(bf16[16,8,128,128]{3,2,0,1:T(8,128)(2,1)} %get-tuple-element.44), calls=%async_computation.3 | async-start | bytes 8388608 | tf_op jit(solution)/shard_map/all_to_all | solution.py:84
  260.9 121.1 %reduce-scatter.2.cloned.1.call-start = ((), (), s32[]{:S(2)}) async-start(), calls=%async_computation.5 | async-start | bytes 6291456 | tf_op jit(solution)/shard_map/reduce_scatter | solution.py:115
Sparse Core Ops, SparseCore 0:
  371.0 10.9 reduce-scatter.1
where the time goes:
time: 394 us; the launch traced here: 392 us
  waiting for transfers between devices  189 us (48%)
  local copies, waits for them, and re-layouts  85.9 us (22%)
  matrix products  53.8 us (14%)
  other arithmetic  19.3 us (5%)
  starting transfers between devices  18.2 us (5%)
  between operations  13.7 us (3%)
  blocking collectives  10.3 us (3%)
    all_to_all x1, waiting for transfers between devices, on_device(): lax.all_to_all(shortened(outputs), 'ctx', split_axis=1, concat_axis=1, ti...  89.5 us
    all_to_all x1, waiting for transfers between devices, on_device(): lax.all_to_all(slot_queries, 'ctx', split_axis=1, concat_axis=1, tiled=True)  88.9 us
    gather x16, local copies, waits for them, and re-layouts, one_portion(): chosen_keys = keys_by_head[head_ids]  31.6 us
    gather x16, local copies, waits for them, and re-layouts, one_portion(): chosen_values = values_by_head[head_ids]  31.6 us
    dot_general x16, matrix products, one_portion(): jnp.einsum('pqd,pkd->pqk', queried, chosen_keys, preferred_element_type=j...  23.6 us
    dot_general x17, matrix products, soft_partial(): jnp.einsum(pattern, weights_low, values_block, preferred_element_type=jnp...  22.1 us
    reduce_scatter x1, waiting for transfers between devices, on_device(): lax.psum_scatter(partial_sums, 'head', scatter_dimension=1, tiled=True)  11.1 us
    all_to_all x1, blocking collectives, on_device(): lax.all_to_all(log_sums, 'ctx', split_axis=1, concat_axis=1, tiled=True)  10.3 us
  transfers between devices with their start and end apart: 4, of which 3 were waited for; matrix products, arithmetic and copies ran while one was open for 4% of the time, Pallas kernels for 0%

commit v1 on v0

--- a/solution.py
+++ b/solution.py
@@ -75,7 +75,12 @@
     outputs, log_sums = lax.map(
         one_portion,
         (
-            lax.all_to_all(slot_queries, "ctx", split_axis=1, concat_axis=1, tiled=True),
+            jnp.concatenate(
+                lax.all_to_all(
+                    jnp.stack(jnp.split(slot_queries, lax.axis_size("ctx"), axis=1)), "ctx", 0, 0
+                ),
+                axis=1,
+            ),
             lax.all_to_all(slot_heads, "ctx", split_axis=1, concat_axis=1, tiled=True),
         ),
     )

time: 394 us -> 399 us (1.013)
  local copies, waits for them, and re-layouts: 85.9 us -> 92.6 us
    unnamed x18 -> x25, local copies, waits for them, and re-layouts: 3.96 us -> 9.98 us
  transfers between devices with their start and end apart: 4 -> 4, of which waited for: 3 -> 3; matrix products, arithmetic and copies ran while one was open for 4% -> 5% of each run, Pallas kernels for 0% -> 0%
where the time goes in v1:
time: 399 us; the launch traced here: 397 us
  waiting for transfers between devices  189 us (47%)
  local copies, waits for them, and re-layouts  92.6 us (23%)
  matrix products  53.8 us (13%)
  starting transfers between devices  18.2 us (5%)
  other arithmetic  18.1 us (5%)
  between operations  13.7 us (3%)
  blocking collectives  10.3 us (3%)
    all_to_all x1, waiting for transfers between devices, on_device(): lax.all_to_all(shortened(outputs), 'ctx', split_axis=1, concat_axis=1, ti...  89.5 us
    all_to_all x1, waiting for transfers between devices, on_device(): lax.all_to_all(jnp.stack(jnp.split(slot_queries, lax.axis_size('ctx'), ax...  88.9 us
    gather x16, local copies, waits for them, and re-layouts, one_portion(): chosen_keys = keys_by_head[head_ids]  31.6 us
    gather x16, local copies, waits for them, and re-layouts, one_portion(): chosen_values = values_by_head[head_ids]  31.6 us
    dot_general x16, matrix products, one_portion(): jnp.einsum('pqd,pkd->pqk', queried, chosen_keys, preferred_element_type=j...  23.6 us
    dot_general x17, matrix products, soft_partial(): jnp.einsum(pattern, weights_low, values_block, preferred_element_type=jnp...  22.1 us
    reduce_scatter x1, waiting for transfers between devices, on_device(): lax.psum_scatter(partial_sums, 'head', scatter_dimension=1, tiled=True)  11.1 us
    all_to_all x1, blocking collectives, on_device(): lax.all_to_all(log_sums, 'ctx', split_axis=1, concat_axis=1, tiled=True)  10.3 us
  transfers between devices with their start and end apart: 4, of which 3 were waited for; matrix products, arithmetic and copies ran while one was open for 5% of the time, Pallas kernels for 0%

profile of v1, /device:TPU:0, one launch (start us, length us, event | category | flops | bytes accessed | tf_op | source)
XLA Modules:
  0.0 397.1 jit_solution(585826026625413593)
XLA Ops:
  10.0 7.3 %all-to-all-start.1 = ((s32[16,8,1]{0,2,1:T(1,128)}), s32[16,8,1]{0,2,1:T(1,128)S(1)}, u32[]{:S(2)}, u32[]{:S(2)}) async-start(s32[16,8,1]{0,2,1:T(1,128)} %copy.135), calls=%async_computation.1 | async-start | bytes 8192 | tf_op jit(solution)/shard_map/all_to_all | solution.py:84
  20.7 3.1 gather_fusion.4
  23.7 2.5 broadcast_select_fusion
  33.2 6.1 %all-to-all-start = ((bf16[8,16,1,128,128]{4,3,1,2,0:T(8,128)(2,1)}), bf16[8,16,1,128,128]{4,3,1,2,0:T(8,128)(2,1)}, u32[]{:S(2)}, u32[]{:S(2)}) async-start(bf16[8,16,1,128,128]{4,3,1,2,0:T(8,128)(2,1)} %fusion.18), calls=%async_computation | async-start | bytes 8388608 | tf_op jit(solution)/shard_map/all_to_all | solution.py:79
  43.2 88.9 %all-to-all-done = bf16[8,16,1,128,128]{4,3,1,2,0:T(8,128)(2,1)} async-done(((bf16[8,16,1,128,128]{4,3,1,2,0:T(8,128)(2,1)}), bf16[8,16,1,128,128]{4,3,1,2,0:T(8,128)(2,1)}, u32[]{:S(2)}, u32[]{:S(2)}) %all-to-all-start) | async-done | bytes 4194336 | tf_op jit(solution)/shard_map/all_to_all | solution.py:79
  132.0 119.4 %while.12 = (s32[]{:T(128)}, bf16[16,8,128,128]{3,2,0,1:T(8,128)(2,1)}, f32[16,8,128]{2,0,1:T(8,128)S(1)}, bf16[16,8,128,128]{3,2,0,1:T(8,128)(2,1)}, s32[16,8]{...) while((s32[]{:T(128)}, ...), condition=%wide.region_7.8_spmd, body=%wide.region_4.7_spmd.sunk | while | flops 273285152 | bytes 13153541 | solution.py:75
  132.0 2.0 gather_fusion.1
  136.1 2.0 gather_fusion
  139.5 2.0 gather_fusion.1
  143.5 2.0 gather_fusion
  146.9 2.0 gather_fusion.1
  151.0 2.0 gather_fusion
  154.4 2.0 gather_fusion.1
  158.4 2.0 gather_fusion
  161.9 2.0 gather_fusion.1
  165.9 2.0 gather_fusion
  169.3 2.0 gather_fusion.1
  171.3 1.5 multiply_reduce_fusion.3
  173.4 2.0 gather_fusion
  176.8 2.0 gather_fusion.1
  180.8 2.0 gather_fusion
  184.2 2.0 gather_fusion.1
  188.3 2.0 gather_fusion
  191.7 2.0 gather_fusion.1
  195.7 2.0 gather_fusion
  199.2 2.0 gather_fusion.1
  203.2 2.0 gather_fusion
  206.6 2.0 gather_fusion.1
  210.7 2.0 gather_fusion
  214.1 2.0 gather_fusion.1
  218.1 2.0 gather_fusion
  221.6 2.0 gather_fusion.1
  225.6 2.0 gather_fusion
  229.0 2.0 gather_fusion.1
  233.1 2.0 gather_fusion
  236.5 2.0 gather_fusion.1
  240.5 2.0 gather_fusion
  244.0 2.0 gather_fusion.1
  248.0 2.0 gather_fusion
  251.4 10.3 %all_to_all.24 = f32[16,8,128]{2,0,1:T(8,128)S(1)} all-to-all(f32[16,8,128]{2,0,1:T(8,128)S(1)} %get-tuple-element.43), channel_id=1, replica_groups=mesh['groups'=2,'ctx'=8,'head'=2] {'ctx'}, dimensions={1} | all-to-all | bytes 131072 | tf_op jit(solution)/shard_map/all_to_all | solution.py:92
  261.7 4.7 %all-to-all-start.3 = ((bf16[16,8,128,128]{3,2,0,1:T(8,128)(2,1)}), bf16[16,8,128,128]{3,2,0,1:T(8,128)(2,1)}, u32[]{:S(2)}, u32[]{:S(2)}) async-start(bf16[16,8,128,128]{3,2,0,1:T(8,128)(2,1)} %get-tuple-element.44), calls=%async_computation.3 | async-start | bytes 8388608 | tf_op jit(solution)/shard_map/all_to_all | solution.py:89
  269.2 89.5 %all-to-all-done.3 = bf16[16,8,128,128]{3,2,0,1:T(8,128)(2,1)} async-done(((bf16[16,8,128,128]{3,2,0,1:T(8,128)(2,1)}), bf16[16,8,128,128]{3,2,0,1:T(8,128)(2,1)}, u32[]{:S(2)}, u32[]{:S(2)}) %all-to-all-start.3) | async-done | bytes 4194336 | tf_op jit(solution)/shard_map/all_to_all | solution.py:89
  358.7 4.7 %copy.149 = bf16[16,8,128,128]{3,2,1,0:T(8,128)(2,1)} copy(bf16[16,8,128,128]{3,2,0,1:T(8,128)(2,1)} %all-to-all-done.3) | data formatting | bytes 8388608 | tf_op jit(solution)/shard_map/all_to_all | solution.py:89
  363.5 3.1 gather_fusion.6
  366.6 1.8 multiply_reduce_fusion.1
  368.8 7.6 %fusion.15 = f32[256,4096]{1,0:T(8,128)} fusion(bf16[1024,4096]{1,0:T(8,128)(2,1)} %param.15, bf16[32,8,8,128]{3,2,1,0:T(8,128)(2,1)S(1)} %bitcast.158), kind=kOutput, calls=%fused_computation.36 | convolution fusion | flops 2147483648 | bytes 13107200 | tf_op jit(solution)/shard_map/dot_general | solution.py:119
  376.4 11.1 %reduce-scatter.2.cloned.1.call-done = f32[256,2048]{1,0:T(8,128)} async-done(((f32[256,4096]{1,0:T(8,128)}), f32[256,2048]{1,0:T(8,128)}) %reduce-scatter.2.cloned.1.call-update) | async-done | bytes 2097168 | tf_op jit(solution)/shard_map/reduce_scatter | solution.py:120
  387.5 2.7 convert_element_type.43
  (177 shorter events, 74.3 us)
Async XLA Ops:
  10.0 23.2 %all-to-all-start.1 = ((s32[16,8,1]{0,2,1:T(1,128)}), s32[16,8,1]{0,2,1:T(1,128)S(1)}, u32[]{:S(2)}, u32[]{:S(2)}) async-start(s32[16,8,1]{0,2,1:T(1,128)} %copy.135), calls=%async_computation.1 | async-start | bytes 8192 | tf_op jit(solution)/shard_map/all_to_all | solution.py:84
  19.8 0.8 copy-start
  33.1 6.2 %copy-start.2 = (bf16[512,1024]{1,0:T(8,128)(2,1)S(1)}, bf16[512,1024]{1,0:T(8,128)(2,1)}, u32[]{:S(2)}) copy-start(bf16[512,1024]{1,0:T(8,128)(2,1)} %param.12) | copy-start | bytes 3145732
  33.2 98.9 %all-to-all-start = ((bf16[8,16,1,128,128]{4,3,1,2,0:T(8,128)(2,1)}), bf16[8,16,1,128,128]{4,3,1,2,0:T(8,128)(2,1)}, u32[]{:S(2)}, u32[]{:S(2)}) async-start(bf16[8,16,1,128,128]{4,3,1,2,0:T(8,128)(2,1)} %fusion.18), calls=%async_computation | async-start | bytes 8388608 | tf_op jit(solution)/shard_map/all_to_all | solution.py:79
  39.3 1.9 copy-start.3
  261.7 4.8 %copy-start.4 = (bf16[256,1024]{1,0:T(8,128)(2,1)S(1)}, bf16[256,1024]{1,0:T(8,128)(2,1)}, u32[]{:S(2)}) copy-start(bf16[256,1024]{1,0:T(8,128)(2,1)} %param.10) | copy-start | bytes 1572868
  261.7 4.9 %copy-start.5 = (bf16[256,1024]{1,0:T(8,128)(2,1)S(1)}, bf16[256,1024]{1,0:T(8,128)(2,1)}, u32[]{:S(2)}) copy-start(bf16[256,1024]{1,0:T(8,128)(2,1)} %param.11) | copy-start | bytes 1572868
  261.7 5.1 %copy-start.1 = (bf16[32,8,8,128]{3,2,1,0:T(8,128)(2,1)S(1)}, bf16[32,8,8,128]{3,2,1,0:T(8,128)(2,1)}, u32[]{:S(2)}) copy-start(bf16[32,8,8,128]{3,2,1,0:T(8,128)(2,1)} %copy-done) | copy-start | bytes 1572868
  261.7 97.0 %all-to-all-start.3 = ((bf16[16,8,128,128]{3,2,0,1:T(8,128)(2,1)}), bf16[16,8,128,128]{3,2,0,1:T(8,128)(2,1)}, u32[]{:S(2)}, u32[]{:S(2)}) async-start(bf16[16,8,128,128]{3,2,0,1:T(8,128)(2,1)} %get-tuple-element.44), calls=%async_computation.3 | async-start | bytes 8388608 | tf_op jit(solution)/shard_map/all_to_all | solution.py:89
  266.4 121.1 %reduce-scatter.2.cloned.1.call-start = ((), (), s32[]{:S(2)}) async-start(), calls=%async_computation.5 | async-start | bytes 6291456 | tf_op jit(solution)/shard_map/reduce_scatter | solution.py:120
Sparse Core Ops, SparseCore 0:
  376.6 10.9 reduce-scatter.1
